TPU v7x, 128 devices: a whole 4x4x4 slice. The times are simulated.
128 devices in a mesh: grp: 16 (over x, y), chan: 8 (over z, core).
Axes of the slice: x: 4, y: 4, z: 4, core: 2. Of those that a mesh axis runs over, the one named last changes fastest.
Arguments:
- spectra: bfloat16 [2048, 2, 2, 8192], P(('grp', 'chan')), may hold values from -45 to 45
- pair_blocks: int32 [16, 8, 18, 2], P('grp', 'chan'), may hold values from 0 to 63
- owners: int32 [16, 8, 18, 1], P('grp', 'chan'), may hold values from 0 to 15; in each aligned block of 18 rows (0 to 17, 18 to 35, ..., all dimensions but the last counted through in order) at most 3 rows name the same one
Outputs:
- stacks: float32 [16, 8, 48, 4, 1024], P('grp', 'chan')
Inputs may be any that keep to these rules, and one draw needn't show every extreme that they name: `owners`: at most 3 of one device's 18 pair blocks name the same owner.
All inputs are finite; a program needn't handle non-finite values.
Results may differ from a plain program's by a relative error of at most 0.011.
Values may be sent and summed in bfloat16 or wider, within the bound.
A program may use at most 128 MiB of HBM per device.

v0:
```python
import jax
import jax.numpy as jnp
from jax import lax
from jax.sharding import PartitionSpec as P

F = 8192
LAGS = 1024
BLK = 2
NB_SRC = 18
MOST = 3
WINDOWS = 2


def table_block(start, count):
    bins = start + jnp.arange(count, dtype=jnp.int32)
    lag_index = jnp.arange(LAGS, dtype=jnp.int32) - LAGS // 2
    phase = bins[:, None] * lag_index[None, :] % (2 * F)
    angle = phase.astype(jnp.float32) * (jnp.pi / F)
    weight = jnp.where(bins == 0, 1.0, 2.0).astype(jnp.float32) / jnp.sqrt(jnp.float32(F))
    cos_part = (jnp.cos(angle) * weight[:, None]).astype(jnp.bfloat16)
    sin_part = (-jnp.sin(angle) * weight[:, None]).astype(jnp.bfloat16)
    return (cos_part, sin_part)


def to_lags(rows):
    width_block = min(512, F)
    real_rows = rows[:, 0]
    imag_rows = rows[:, 1]

    def add_block(turn, total):
        start = (turn * width_block).astype(jnp.int32)
        cos_part, sin_part = table_block(start, width_block)
        real_slice = lax.dynamic_slice_in_dim(real_rows, start, width_block, 1)
        imag_slice = lax.dynamic_slice_in_dim(imag_rows, start, width_block, 1)
        total = total + jnp.dot(real_slice, cos_part, preferred_element_type=jnp.float32)
        return total + jnp.dot(imag_slice, sin_part, preferred_element_type=jnp.float32)

    start_total = jnp.zeros((rows.shape[0], LAGS), jnp.float32)
    return lax.fori_loop(0, F // width_block, add_block, start_total)


def whiten(spectra):
    values = spectra.astype(jnp.float32)
    power = values[:, :, 0] ** 2 + values[:, :, 1] ** 2
    level = jnp.mean(power, axis=-1, keepdims=True) + 1e-05
    scale = lax.rsqrt(power + 0.1 * level)
    return (values * scale[:, :, None, :]).astype(jnp.bfloat16)


def cross_pairs(left, right):
    real_left = left[..., :, None, :, 0, :]
    imag_left = left[..., :, None, :, 1, :]
    real_right = right[..., None, :, :, 0, :]
    imag_right = right[..., None, :, :, 1, :]
    real_part = real_left * real_right + imag_left * imag_right
    imag_part = imag_left * real_right - real_left * imag_right
    both = jnp.stack([real_part, imag_part], axis=-2)
    return both.astype(jnp.bfloat16)


def local(spectra, pair_blocks, owners):
    groups_count = lax.axis_size("grp")
    slot_count = groups_count * MOST
    white = whiten(spectra)
    panel = lax.all_gather(white, "chan", axis=0, tiled=True)
    blocks = pair_blocks[0, 0]
    offsets = jnp.arange(BLK, dtype=jnp.int32)
    left_idx = blocks[:, 0][:, None] * BLK + offsets
    right_idx = blocks[:, 1][:, None] * BLK + offsets
    left = jnp.take(panel, left_idx, axis=0).astype(jnp.float32)
    right = jnp.take(panel, right_idx, axis=0).astype(jnp.float32)
    cross = cross_pairs(left, right).reshape(NB_SRC, BLK * BLK, WINDOWS, 2, F)
    owner_list = owners[0, 0, :, 0]
    same = owner_list[:, None] == owner_list[None, :]
    earlier = jnp.arange(NB_SRC)[None, :] < jnp.arange(NB_SRC)[:, None]
    order_rank = jnp.sum(jnp.logical_and(same, earlier), axis=1)
    slot_ids = owner_list * MOST + order_rank
    chooser = slot_ids[None, :] == jnp.arange(slot_count, dtype=jnp.int32)[:, None]
    pairs = BLK * BLK
    summed = jnp.zeros((groups_count, MOST, pairs, 2, F), jnp.float32)
    for window in range(WINDOWS):
        placed = jnp.einsum(
            "ms,sprf->mprf",
            chooser.astype(jnp.bfloat16),
            cross[:, :, window],
            preferred_element_type=jnp.float32,
        )
        summed = summed + lax.all_to_all(
            placed.astype(jnp.bfloat16).reshape(groups_count, MOST, pairs, 2, F),
            "grp",
            split_axis=0,
            concat_axis=0,
            tiled=True,
        ).astype(jnp.float32)
    received = (summed / WINDOWS).astype(jnp.bfloat16)
    shape_now = received.shape
    rows = received.reshape(-1, 2, F)
    result = to_lags(rows).reshape(shape_now[0], shape_now[1], pairs, LAGS)
    return result.reshape(1, 1, slot_count, pairs, LAGS)


def solution(mesh):
    return jax.shard_map(
        local,
        mesh=mesh,
        in_specs=(
            P(("grp", "chan"), None, None, None),
            P("grp", "chan", None, None),
            P("grp", "chan", None, None),
        ),
        out_specs=P("grp", "chan", None, None, None),
        check_vma=False,
    )
```

profile of v0, /device:TPU:20, one launch (start us, length us, event | category | flops | bytes accessed | tf_op | source)
XLA Modules:
  0.0 685.6 jit_solution(13492980502422854776)
XLA Ops:
  13.3 51.4 %all-gather.2.cloned.1.call-done = bf16[128,2,2,8192]{3,2,1,0:T(2,128)(2,1)} async-done(((bf16[16,2,2,8192]{3,2,1,0:T(2,128)(2,1)}), bf16[128,2,2,8192]{3,2,1,0:T(2,128)(2,1)}) %all-gather.2.cloned.1.call-update) | async-done | bytes 8388624 | tf_op jit(solution)/shard_map/all_gather | solution.py:65
  64.7 11.3 %gather_fusion = bf16[36,2,2,8192]{3,2,1,0:T(2,128)(2,1)S(1)} fusion(bf16[128,2,2,8192]{3,2,1,0:T(2,128)(2,1)} %all-gather.2.cloned.1.call-done, s32[1024]{0:T(1024)S(1)} %pad_clamp_fusion.1), kind=kCustom, calls=%fused_computation.clone | custom fusion | bytes 4718736 | tf_op jit(solution)/shard_map/jit(_take)/gather | solution.py:70
  78.1 5.4 fusion.36
  90.0 11.5 %gather_fusion.1 = bf16[36,2,2,8192]{3,2,1,0:T(2,128)(2,1)S(1)} fusion(bf16[128,2,2,8192]{3,2,1,0:T(2,128)(2,1)} %all-gather.2.cloned.1.call-done, s32[1024]{0:T(1024)S(1)} %pad_clamp_fusion), kind=kCustom, calls=%fused_computation.1.clone | custom fusion | bytes 4718736 | tf_op jit(solution)/shard_map/jit(_take)/gather | solution.py:71
  103.6 5.4 fusion.37
  116.5 11.0 %copy.58 = bf16[48,4,2,8192]{3,2,1,0:T(2,128)(2,1)} copy(bf16[48,4,2,8192]{3,0,2,1:T(8,128)(2,1)S(1)} %convolution_convert_fusion.1) | data formatting | bytes 12582912 | tf_op jit(solution)/shard_map/convert_element_type | solution.py:89
  127.5 7.2 %all-to-all-start = ((bf16[16,3,4,2,8192]{4,3,2,1,0:T(2,128)(2,1)}), bf16[16,3,4,2,8192]{4,3,2,1,0:T(2,128)(2,1)}, u32[]{:S(2)}, u32[]{:S(2)}) async-start(bf16[16,3,4,2,8192]{4,3,2,1,0:T(2,128)(2,1)} %bitcast.52), calls=%async_computation | async-start | bytes 12582912 | tf_op jit(solution)/shard_map/all_to_all | solution.py:88
  138.0 11.0 %copy.59 = bf16[48,4,2,8192]{3,2,1,0:T(2,128)(2,1)} copy(bf16[48,4,2,8192]{3,0,2,1:T(8,128)(2,1)S(1)} %convolution_convert_fusion) | data formatting | bytes 12582912 | tf_op jit(solution)/shard_map/convert_element_type | solution.py:89
  149.0 89.4 %all-to-all-done = bf16[16,3,4,2,8192]{4,3,2,1,0:T(2,128)(2,1)} async-done(((bf16[16,3,4,2,8192]{4,3,2,1,0:T(2,128)(2,1)}), bf16[16,3,4,2,8192]{4,3,2,1,0:T(2,128)(2,1)}, u32[]{:S(2)}, u32[]{:S(2)}) %all-to-all-start) | async-done | bytes 6291488 | tf_op jit(solution)/shard_map/all_to_all | solution.py:88
  238.5 14.3 %all-to-all-start.1 = ((bf16[16,3,4,2,8192]{4,3,2,1,0:T(2,128)(2,1)}), bf16[16,3,4,2,8192]{4,3,2,1,0:T(2,128)(2,1)}, u32[]{:S(2)}, u32[]{:S(2)}) async-start(bf16[16,3,4,2,8192]{4,3,2,1,0:T(2,128)(2,1)} %bitcast.51), calls=%async_computation.1 | async-start | bytes 12582912 | tf_op jit(solution)/shard_map/all_to_all | solution.py:88
  252.8 99.9 %all-to-all-done.1 = bf16[16,3,4,2,8192]{4,3,2,1,0:T(2,128)(2,1)} async-done(((bf16[16,3,4,2,8192]{4,3,2,1,0:T(2,128)(2,1)}), bf16[16,3,4,2,8192]{4,3,2,1,0:T(2,128)(2,1)}, u32[]{:S(2)}, u32[]{:S(2)}) %all-to-all-start.1) | async-done | bytes 6291488 | tf_op jit(solution)/shard_map/all_to_all | solution.py:88
  352.7 11.2 %multiply_convert_fusion.4 = bf16[16,3,4,2,8192]{4,3,2,1,0:T(2,128)(2,1)S(1)} fusion(bf16[16,3,4,2,8192]{4,3,2,1,0:T(2,128)(2,1)} %all-to-all-done.1, bf16[16,3,4,2,8192]{4,3,2,1,0:T(2,128)(2,1)} %all-to-all-done), kind=kLoop, calls=%fused_computation.29 | loop fusion | flops 15728640 | bytes 18874368 | tf_op jit(solution)/shard_map/convert_element_type | solution.py:95
  363.9 13.4 %fusion.35 = (bf16[192,1,8192]{2,1,0:T(2,128)(2,1)S(1)}, bf16[192,1,8192]{2,1,0:T(2,128)(2,1)S(1)}) fusion(bf16[192,2,8192]{2,1,0:T(2,128)(2,1)S(1)} %bitcast.46), kind=kLoop, calls=%fused_computation.77 | loop fusion | bytes 12582912 | tf_op jit(solution)/shard_map/slice | solution.py:28
  377.3 3.4 copy.78
  380.8 5.1 copy.79
  385.9 290.4 %while.16 = (s32[]{:T(128)}, f32[192,1024]{1,0:T(8,128)}, bf16[192,8192]{1,0:T(8,128)(2,1)}, bf16[192,8192]{1,0:T(8,128)(2,1)S(1)}, s32[]{:T(128)}, /*index=5*/s32[]{:T(128)}, s32[]{:T(128)}, s32[]{:T(128)}) while((s32[]{:T(128)}, f32[192,1024]{1,0:T(8,128)}, bf16[192,8192]{1,0:T(8,128)(2,1)}, bf16[192,8192]{1,0:T(8,128)(2,1)S(1)}, ...), condition=%wide.region_3.5_spmd.clone, body=%wide.region_2.4_spmd.clone.sunk | while | flops 420548096 | bytes 3563677 | solution.py:39
  386.1 8.9 %convolution_add_fusion.4 = f32[192,1024]{1,0:T(8,128)S(1)} fusion(f32[512]{0:T(512)S(1)} %select_multiply_fusion.2, s32[1024]{0:T(1024)S(1)} %iota_add_fusion.4, s32[512]{0:T(512)S(1)} %iota_add_fusion.5, f32[192,1024]{1,0:T(8,128)} %get-tuple-element.190, pred[]{:T(512)S(6)} %compare.4, bf16[192,8192]{1,0:T(8,128)(2,1)} %get-tuple-element.199, ...), kind=kOutput, calls=%fused_computation.13.clone.1 | convolution fusion | flops 210108416 | bytes 1777669 | tf_op jit(solution)/shard_map/while/body/eval_jaxpr/dot_general | solution.py:35
  395.0 9.0 %convolution_add_fusion.5 = f32[192,1024]{1,0:T(8,128)} fusion(f32[192,1024]{1,0:T(8,128)S(1)} %convolution_add_fusion.4, f32[512]{0:T(512)S(1)} %select_multiply_fusion.2, s32[1024]{0:T(1024)S(1)} %iota_add_fusion.4, s32[512]{0:T(512)S(1)} %iota_add_fusion.5, bf16[192,8192]{1,0:T(8,128)(2,1)S(1)} %get-tuple-element.200, s32[]{:T(128)S(6)} %select_n.93), kind=kOutput, calls=%fused_computation.12.clone.1 | convolution fusion | flops 210436096 | bytes 1777668 | tf_op jit(solution)/shard_map/while/body/eval_jaxpr/dot_general | solution.py:36
  403.9 9.2 %convolution_add_fusion.4 = f32[192,1024]{1,0:T(8,128)S(1)} fusion(f32[512]{0:T(512)S(1)} %select_multiply_fusion.2, s32[1024]{0:T(1024)S(1)} %iota_add_fusion.4, s32[512]{0:T(512)S(1)} %iota_add_fusion.5, f32[192,1024]{1,0:T(8,128)} %get-tuple-element.190, pred[]{:T(512)S(6)} %compare.4, bf16[192,8192]{1,0:T(8,128)(2,1)} %get-tuple-element.199, ...), kind=kOutput, calls=%fused_computation.13.clone.1 | convolution fusion | flops 210108416 | bytes 1777669 | tf_op jit(solution)/shard_map/while/body/eval_jaxpr/dot_general | solution.py:35
  413.1 9.0 %convolution_add_fusion.5 = f32[192,1024]{1,0:T(8,128)} fusion(f32[192,1024]{1,0:T(8,128)S(1)} %convolution_add_fusion.4, f32[512]{0:T(512)S(1)} %select_multiply_fusion.2, s32[1024]{0:T(1024)S(1)} %iota_add_fusion.4, s32[512]{0:T(512)S(1)} %iota_add_fusion.5, bf16[192,8192]{1,0:T(8,128)(2,1)S(1)} %get-tuple-element.200, s32[]{:T(128)S(6)} %select_n.93), kind=kOutput, calls=%fused_computation.12.clone.1 | convolution fusion | flops 210436096 | bytes 1777668 | tf_op jit(solution)/shard_map/while/body/eval_jaxpr/dot_general | solution.py:36
  422.1 9.2 %convolution_add_fusion.4 = f32[192,1024]{1,0:T(8,128)S(1)} fusion(f32[512]{0:T(512)S(1)} %select_multiply_fusion.2, s32[1024]{0:T(1024)S(1)} %iota_add_fusion.4, s32[512]{0:T(512)S(1)} %iota_add_fusion.5, f32[192,1024]{1,0:T(8,128)} %get-tuple-element.190, pred[]{:T(512)S(6)} %compare.4, bf16[192,8192]{1,0:T(8,128)(2,1)} %get-tuple-element.199, ...), kind=kOutput, calls=%fused_computation.13.clone.1 | convolution fusion | flops 210108416 | bytes 1777669 | tf_op jit(solution)/shard_map/while/body/eval_jaxpr/dot_general | solution.py:35
  431.3 9.0 %convolution_add_fusion.5 = f32[192,1024]{1,0:T(8,128)} fusion(f32[192,1024]{1,0:T(8,128)S(1)} %convolution_add_fusion.4, f32[512]{0:T(512)S(1)} %select_multiply_fusion.2, s32[1024]{0:T(1024)S(1)} %iota_add_fusion.4, s32[512]{0:T(512)S(1)} %iota_add_fusion.5, bf16[192,8192]{1,0:T(8,128)(2,1)S(1)} %get-tuple-element.200, s32[]{:T(128)S(6)} %select_n.93), kind=kOutput, calls=%fused_computation.12.clone.1 | convolution fusion | flops 210436096 | bytes 1777668 | tf_op jit(solution)/shard_map/while/body/eval_jaxpr/dot_general | solution.py:36
  440.2 9.2 %convolution_add_fusion.4 = f32[192,1024]{1,0:T(8,128)S(1)} fusion(f32[512]{0:T(512)S(1)} %select_multiply_fusion.2, s32[1024]{0:T(1024)S(1)} %iota_add_fusion.4, s32[512]{0:T(512)S(1)} %iota_add_fusion.5, f32[192,1024]{1,0:T(8,128)} %get-tuple-element.190, pred[]{:T(512)S(6)} %compare.4, bf16[192,8192]{1,0:T(8,128)(2,1)} %get-tuple-element.199, ...), kind=kOutput, calls=%fused_computation.13.clone.1 | convolution fusion | flops 210108416 | bytes 1777669 | tf_op jit(solution)/shard_map/while/body/eval_jaxpr/dot_general | solution.py:35
  449.4 9.0 %convolution_add_fusion.5 = f32[192,1024]{1,0:T(8,128)} fusion(f32[192,1024]{1,0:T(8,128)S(1)} %convolution_add_fusion.4, f32[512]{0:T(512)S(1)} %select_multiply_fusion.2, s32[1024]{0:T(1024)S(1)} %iota_add_fusion.4, s32[512]{0:T(512)S(1)} %iota_add_fusion.5, bf16[192,8192]{1,0:T(8,128)(2,1)S(1)} %get-tuple-element.200, s32[]{:T(128)S(6)} %select_n.93), kind=kOutput, calls=%fused_computation.12.clone.1 | convolution fusion | flops 210436096 | bytes 1777668 | tf_op jit(solution)/shard_map/while/body/eval_jaxpr/dot_general | solution.py:36
  458.4 9.2 %convolution_add_fusion.4 = f32[192,1024]{1,0:T(8,128)S(1)} fusion(f32[512]{0:T(512)S(1)} %select_multiply_fusion.2, s32[1024]{0:T(1024)S(1)} %iota_add_fusion.4, s32[512]{0:T(512)S(1)} %iota_add_fusion.5, f32[192,1024]{1,0:T(8,128)} %get-tuple-element.190, pred[]{:T(512)S(6)} %compare.4, bf16[192,8192]{1,0:T(8,128)(2,1)} %get-tuple-element.199, ...), kind=kOutput, calls=%fused_computation.13.clone.1 | convolution fusion | flops 210108416 | bytes 1777669 | tf_op jit(solution)/shard_map/while/body/eval_jaxpr/dot_general | solution.py:35
  467.6 9.0 %convolution_add_fusion.5 = f32[192,1024]{1,0:T(8,128)} fusion(f32[192,1024]{1,0:T(8,128)S(1)} %convolution_add_fusion.4, f32[512]{0:T(512)S(1)} %select_multiply_fusion.2, s32[1024]{0:T(1024)S(1)} %iota_add_fusion.4, s32[512]{0:T(512)S(1)} %iota_add_fusion.5, bf16[192,8192]{1,0:T(8,128)(2,1)S(1)} %get-tuple-element.200, s32[]{:T(128)S(6)} %select_n.93), kind=kOutput, calls=%fused_computation.12.clone.1 | convolution fusion | flops 210436096 | bytes 1777668 | tf_op jit(solution)/shard_map/while/body/eval_jaxpr/dot_general | solution.py:36
  476.6 9.2 %convolution_add_fusion.4 = f32[192,1024]{1,0:T(8,128)S(1)} fusion(f32[512]{0:T(512)S(1)} %select_multiply_fusion.2, s32[1024]{0:T(1024)S(1)} %iota_add_fusion.4, s32[512]{0:T(512)S(1)} %iota_add_fusion.5, f32[192,1024]{1,0:T(8,128)} %get-tuple-element.190, pred[]{:T(512)S(6)} %compare.4, bf16[192,8192]{1,0:T(8,128)(2,1)} %get-tuple-element.199, ...), kind=kOutput, calls=%fused_computation.13.clone.1 | convolution fusion | flops 210108416 | bytes 1777669 | tf_op jit(solution)/shard_map/while/body/eval_jaxpr/dot_general | solution.py:35
  485.7 9.0 %convolution_add_fusion.5 = f32[192,1024]{1,0:T(8,128)} fusion(f32[192,1024]{1,0:T(8,128)S(1)} %convolution_add_fusion.4, f32[512]{0:T(512)S(1)} %select_multiply_fusion.2, s32[1024]{0:T(1024)S(1)} %iota_add_fusion.4, s32[512]{0:T(512)S(1)} %iota_add_fusion.5, bf16[192,8192]{1,0:T(8,128)(2,1)S(1)} %get-tuple-element.200, s32[]{:T(128)S(6)} %select_n.93), kind=kOutput, calls=%fused_computation.12.clone.1 | convolution fusion | flops 210436096 | bytes 1777668 | tf_op jit(solution)/shard_map/while/body/eval_jaxpr/dot_general | solution.py:36
  494.7 9.2 %convolution_add_fusion.4 = f32[192,1024]{1,0:T(8,128)S(1)} fusion(f32[512]{0:T(512)S(1)} %select_multiply_fusion.2, s32[1024]{0:T(1024)S(1)} %iota_add_fusion.4, s32[512]{0:T(512)S(1)} %iota_add_fusion.5, f32[192,1024]{1,0:T(8,128)} %get-tuple-element.190, pred[]{:T(512)S(6)} %compare.4, bf16[192,8192]{1,0:T(8,128)(2,1)} %get-tuple-element.199, ...), kind=kOutput, calls=%fused_computation.13.clone.1 | convolution fusion | flops 210108416 | bytes 1777669 | tf_op jit(solution)/shard_map/while/body/eval_jaxpr/dot_general | solution.py:35
  503.9 9.0 %convolution_add_fusion.5 = f32[192,1024]{1,0:T(8,128)} fusion(f32[192,1024]{1,0:T(8,128)S(1)} %convolution_add_fusion.4, f32[512]{0:T(512)S(1)} %select_multiply_fusion.2, s32[1024]{0:T(1024)S(1)} %iota_add_fusion.4, s32[512]{0:T(512)S(1)} %iota_add_fusion.5, bf16[192,8192]{1,0:T(8,128)(2,1)S(1)} %get-tuple-element.200, s32[]{:T(128)S(6)} %select_n.93), kind=kOutput, calls=%fused_computation.12.clone.1 | convolution fusion | flops 210436096 | bytes 1777668 | tf_op jit(solution)/shard_map/while/body/eval_jaxpr/dot_general | solution.py:36
  512.9 9.2 %convolution_add_fusion.4 = f32[192,1024]{1,0:T(8,128)S(1)} fusion(f32[512]{0:T(512)S(1)} %select_multiply_fusion.2, s32[1024]{0:T(1024)S(1)} %iota_add_fusion.4, s32[512]{0:T(512)S(1)} %iota_add_fusion.5, f32[192,1024]{1,0:T(8,128)} %get-tuple-element.190, pred[]{:T(512)S(6)} %compare.4, bf16[192,8192]{1,0:T(8,128)(2,1)} %get-tuple-element.199, ...), kind=kOutput, calls=%fused_computation.13.clone.1 | convolution fusion | flops 210108416 | bytes 1777669 | tf_op jit(solution)/shard_map/while/body/eval_jaxpr/dot_general | solution.py:35
  522.1 9.0 %convolution_add_fusion.5 = f32[192,1024]{1,0:T(8,128)} fusion(f32[192,1024]{1,0:T(8,128)S(1)} %convolution_add_fusion.4, f32[512]{0:T(512)S(1)} %select_multiply_fusion.2, s32[1024]{0:T(1024)S(1)} %iota_add_fusion.4, s32[512]{0:T(512)S(1)} %iota_add_fusion.5, bf16[192,8192]{1,0:T(8,128)(2,1)S(1)} %get-tuple-element.200, s32[]{:T(128)S(6)} %select_n.93), kind=kOutput, calls=%fused_computation.12.clone.1 | convolution fusion | flops 210436096 | bytes 1777668 | tf_op jit(solution)/shard_map/while/body/eval_jaxpr/dot_general | solution.py:36
  531.0 9.2 %convolution_add_fusion.4 = f32[192,1024]{1,0:T(8,128)S(1)} fusion(f32[512]{0:T(512)S(1)} %select_multiply_fusion.2, s32[1024]{0:T(1024)S(1)} %iota_add_fusion.4, s32[512]{0:T(512)S(1)} %iota_add_fusion.5, f32[192,1024]{1,0:T(8,128)} %get-tuple-element.190, pred[]{:T(512)S(6)} %compare.4, bf16[192,8192]{1,0:T(8,128)(2,1)} %get-tuple-element.199, ...), kind=kOutput, calls=%fused_computation.13.clone.1 | convolution fusion | flops 210108416 | bytes 1777669 | tf_op jit(solution)/shard_map/while/body/eval_jaxpr/dot_general | solution.py:35
  540.2 9.0 %convolution_add_fusion.5 = f32[192,1024]{1,0:T(8,128)} fusion(f32[192,1024]{1,0:T(8,128)S(1)} %convolution_add_fusion.4, f32[512]{0:T(512)S(1)} %select_multiply_fusion.2, s32[1024]{0:T(1024)S(1)} %iota_add_fusion.4, s32[512]{0:T(512)S(1)} %iota_add_fusion.5, bf16[192,8192]{1,0:T(8,128)(2,1)S(1)} %get-tuple-element.200, s32[]{:T(128)S(6)} %select_n.93), kind=kOutput, calls=%fused_computation.12.clone.1 | convolution fusion | flops 210436096 | bytes 1777668 | tf_op jit(solution)/shard_map/while/body/eval_jaxpr/dot_general | solution.py:36
  549.2 9.2 %convolution_add_fusion.4 = f32[192,1024]{1,0:T(8,128)S(1)} fusion(f32[512]{0:T(512)S(1)} %select_multiply_fusion.2, s32[1024]{0:T(1024)S(1)} %iota_add_fusion.4, s32[512]{0:T(512)S(1)} %iota_add_fusion.5, f32[192,1024]{1,0:T(8,128)} %get-tuple-element.190, pred[]{:T(512)S(6)} %compare.4, bf16[192,8192]{1,0:T(8,128)(2,1)} %get-tuple-element.199, ...), kind=kOutput, calls=%fused_computation.13.clone.1 | convolution fusion | flops 210108416 | bytes 1777669 | tf_op jit(solution)/shard_map/while/body/eval_jaxpr/dot_general | solution.py:35
  558.4 9.0 %convolution_add_fusion.5 = f32[192,1024]{1,0:T(8,128)} fusion(f32[192,1024]{1,0:T(8,128)S(1)} %convolution_add_fusion.4, f32[512]{0:T(512)S(1)} %select_multiply_fusion.2, s32[1024]{0:T(1024)S(1)} %iota_add_fusion.4, s32[512]{0:T(512)S(1)} %iota_add_fusion.5, bf16[192,8192]{1,0:T(8,128)(2,1)S(1)} %get-tuple-element.200, s32[]{:T(128)S(6)} %select_n.93), kind=kOutput, calls=%fused_computation.12.clone.1 | convolution fusion | flops 210436096 | bytes 1777668 | tf_op jit(solution)/shard_map/while/body/eval_jaxpr/dot_general | solution.py:36
  567.3 9.2 %convolution_add_fusion.4 = f32[192,1024]{1,0:T(8,128)S(1)} fusion(f32[512]{0:T(512)S(1)} %select_multiply_fusion.2, s32[1024]{0:T(1024)S(1)} %iota_add_fusion.4, s32[512]{0:T(512)S(1)} %iota_add_fusion.5, f32[192,1024]{1,0:T(8,128)} %get-tuple-element.190, pred[]{:T(512)S(6)} %compare.4, bf16[192,8192]{1,0:T(8,128)(2,1)} %get-tuple-element.199, ...), kind=kOutput, calls=%fused_computation.13.clone.1 | convolution fusion | flops 210108416 | bytes 1777669 | tf_op jit(solution)/shard_map/while/body/eval_jaxpr/dot_general | solution.py:35
  576.5 9.0 %convolution_add_fusion.5 = f32[192,1024]{1,0:T(8,128)} fusion(f32[192,1024]{1,0:T(8,128)S(1)} %convolution_add_fusion.4, f32[512]{0:T(512)S(1)} %select_multiply_fusion.2, s32[1024]{0:T(1024)S(1)} %iota_add_fusion.4, s32[512]{0:T(512)S(1)} %iota_add_fusion.5, bf16[192,8192]{1,0:T(8,128)(2,1)S(1)} %get-tuple-element.200, s32[]{:T(128)S(6)} %select_n.93), kind=kOutput, calls=%fused_computation.12.clone.1 | convolution fusion | flops 210436096 | bytes 1777668 | tf_op jit(solution)/shard_map/while/body/eval_jaxpr/dot_general | solution.py:36
  585.5 9.2 %convolution_add_fusion.4 = f32[192,1024]{1,0:T(8,128)S(1)} fusion(f32[512]{0:T(512)S(1)} %select_multiply_fusion.2, s32[1024]{0:T(1024)S(1)} %iota_add_fusion.4, s32[512]{0:T(512)S(1)} %iota_add_fusion.5, f32[192,1024]{1,0:T(8,128)} %get-tuple-element.190, pred[]{:T(512)S(6)} %compare.4, bf16[192,8192]{1,0:T(8,128)(2,1)} %get-tuple-element.199, ...), kind=kOutput, calls=%fused_computation.13.clone.1 | convolution fusion | flops 210108416 | bytes 1777669 | tf_op jit(solution)/shard_map/while/body/eval_jaxpr/dot_general | solution.py:35
  594.7 9.0 %convolution_add_fusion.5 = f32[192,1024]{1,0:T(8,128)} fusion(f32[192,1024]{1,0:T(8,128)S(1)} %convolution_add_fusion.4, f32[512]{0:T(512)S(1)} %select_multiply_fusion.2, s32[1024]{0:T(1024)S(1)} %iota_add_fusion.4, s32[512]{0:T(512)S(1)} %iota_add_fusion.5, bf16[192,8192]{1,0:T(8,128)(2,1)S(1)} %get-tuple-element.200, s32[]{:T(128)S(6)} %select_n.93), kind=kOutput, calls=%fused_computation.12.clone.1 | convolution fusion | flops 210436096 | bytes 1777668 | tf_op jit(solution)/shard_map/while/body/eval_jaxpr/dot_general | solution.py:36
  603.6 9.2 %convolution_add_fusion.4 = f32[192,1024]{1,0:T(8,128)S(1)} fusion(f32[512]{0:T(512)S(1)} %select_multiply_fusion.2, s32[1024]{0:T(1024)S(1)} %iota_add_fusion.4, s32[512]{0:T(512)S(1)} %iota_add_fusion.5, f32[192,1024]{1,0:T(8,128)} %get-tuple-element.190, pred[]{:T(512)S(6)} %compare.4, bf16[192,8192]{1,0:T(8,128)(2,1)} %get-tuple-element.199, ...), kind=kOutput, calls=%fused_computation.13.clone.1 | convolution fusion | flops 210108416 | bytes 1777669 | tf_op jit(solution)/shard_map/while/body/eval_jaxpr/dot_general | solution.py:35
  612.8 9.0 %convolution_add_fusion.5 = f32[192,1024]{1,0:T(8,128)} fusion(f32[192,1024]{1,0:T(8,128)S(1)} %convolution_add_fusion.4, f32[512]{0:T(512)S(1)} %select_multiply_fusion.2, s32[1024]{0:T(1024)S(1)} %iota_add_fusion.4, s32[512]{0:T(512)S(1)} %iota_add_fusion.5, bf16[192,8192]{1,0:T(8,128)(2,1)S(1)} %get-tuple-element.200, s32[]{:T(128)S(6)} %select_n.93), kind=kOutput, calls=%fused_computation.12.clone.1 | convolution fusion | flops 210436096 | bytes 1777668 | tf_op jit(solution)/shard_map/while/body/eval_jaxpr/dot_general | solution.py:36
  621.8 9.2 %convolution_add_fusion.4 = f32[192,1024]{1,0:T(8,128)S(1)} fusion(f32[512]{0:T(512)S(1)} %select_multiply_fusion.2, s32[1024]{0:T(1024)S(1)} %iota_add_fusion.4, s32[512]{0:T(512)S(1)} %iota_add_fusion.5, f32[192,1024]{1,0:T(8,128)} %get-tuple-element.190, pred[]{:T(512)S(6)} %compare.4, bf16[192,8192]{1,0:T(8,128)(2,1)} %get-tuple-element.199, ...), kind=kOutput, calls=%fused_computation.13.clone.1 | convolution fusion | flops 210108416 | bytes 1777669 | tf_op jit(solution)/shard_map/while/body/eval_jaxpr/dot_general | solution.py:35
  631.0 9.0 %convolution_add_fusion.5 = f32[192,1024]{1,0:T(8,128)} fusion(f32[192,1024]{1,0:T(8,128)S(1)} %convolution_add_fusion.4, f32[512]{0:T(512)S(1)} %select_multiply_fusion.2, s32[1024]{0:T(1024)S(1)} %iota_add_fusion.4, s32[512]{0:T(512)S(1)} %iota_add_fusion.5, bf16[192,8192]{1,0:T(8,128)(2,1)S(1)} %get-tuple-element.200, s32[]{:T(128)S(6)} %select_n.93), kind=kOutput, calls=%fused_computation.12.clone.1 | convolution fusion | flops 210436096 | bytes 1777668 | tf_op jit(solution)/shard_map/while/body/eval_jaxpr/dot_general | solution.py:36
  640.0 9.2 %convolution_add_fusion.4 = f32[192,1024]{1,0:T(8,128)S(1)} fusion(f32[512]{0:T(512)S(1)} %select_multiply_fusion.2, s32[1024]{0:T(1024)S(1)} %iota_add_fusion.4, s32[512]{0:T(512)S(1)} %iota_add_fusion.5, f32[192,1024]{1,0:T(8,128)} %get-tuple-element.190, pred[]{:T(512)S(6)} %compare.4, bf16[192,8192]{1,0:T(8,128)(2,1)} %get-tuple-element.199, ...), kind=kOutput, calls=%fused_computation.13.clone.1 | convolution fusion | flops 210108416 | bytes 1777669 | tf_op jit(solution)/shard_map/while/body/eval_jaxpr/dot_general | solution.py:35
  649.1 9.0 %convolution_add_fusion.5 = f32[192,1024]{1,0:T(8,128)} fusion(f32[192,1024]{1,0:T(8,128)S(1)} %convolution_add_fusion.4, f32[512]{0:T(512)S(1)} %select_multiply_fusion.2, s32[1024]{0:T(1024)S(1)} %iota_add_fusion.4, s32[512]{0:T(512)S(1)} %iota_add_fusion.5, bf16[192,8192]{1,0:T(8,128)(2,1)S(1)} %get-tuple-element.200, s32[]{:T(128)S(6)} %select_n.93), kind=kOutput, calls=%fused_computation.12.clone.1 | convolution fusion | flops 210436096 | bytes 1777668 | tf_op jit(solution)/shard_map/while/body/eval_jaxpr/dot_general | solution.py:36
  658.1 9.2 %convolution_add_fusion.4 = f32[192,1024]{1,0:T(8,128)S(1)} fusion(f32[512]{0:T(512)S(1)} %select_multiply_fusion.2, s32[1024]{0:T(1024)S(1)} %iota_add_fusion.4, s32[512]{0:T(512)S(1)} %iota_add_fusion.5, f32[192,1024]{1,0:T(8,128)} %get-tuple-element.190, pred[]{:T(512)S(6)} %compare.4, bf16[192,8192]{1,0:T(8,128)(2,1)} %get-tuple-element.199, ...), kind=kOutput, calls=%fused_computation.13.clone.1 | convolution fusion | flops 210108416 | bytes 1777669 | tf_op jit(solution)/shard_map/while/body/eval_jaxpr/dot_general | solution.py:35
  667.3 9.0 %convolution_add_fusion.5 = f32[192,1024]{1,0:T(8,128)} fusion(f32[192,1024]{1,0:T(8,128)S(1)} %convolution_add_fusion.4, f32[512]{0:T(512)S(1)} %select_multiply_fusion.2, s32[1024]{0:T(1024)S(1)} %iota_add_fusion.4, s32[512]{0:T(512)S(1)} %iota_add_fusion.5, bf16[192,8192]{1,0:T(8,128)(2,1)S(1)} %get-tuple-element.200, s32[]{:T(128)S(6)} %select_n.93), kind=kOutput, calls=%fused_computation.12.clone.1 | convolution fusion | flops 210436096 | bytes 1777668 | tf_op jit(solution)/shard_map/while/body/eval_jaxpr/dot_general | solution.py:36
  (92 shorter events, 30.6 us)
Async XLA Ops:
  6.5 58.1 %all-gather.2.cloned.1.call-start = ((), (), s32[]{:S(2)}) async-start(), calls=%async_computation.2 | async-start | bytes 9437184 | tf_op jit(solution)/shard_map/all_gather | solution.py:65
  8.4 1.2 copy-start.3
  9.6 2.8 copy-start.4
  9.6 3.5 copy-start.5
  109.0 3.1 copy-start.2
  110.6 2.0 copy-start.1
  114.2 2.2 copy-start
  127.5 111.0 %all-to-all-start = ((bf16[16,3,4,2,8192]{4,3,2,1,0:T(2,128)(2,1)}), bf16[16,3,4,2,8192]{4,3,2,1,0:T(2,128)(2,1)}, u32[]{:S(2)}, u32[]{:S(2)}) async-start(bf16[16,3,4,2,8192]{4,3,2,1,0:T(2,128)(2,1)} %bitcast.52), calls=%async_computation | async-start | bytes 12582912 | tf_op jit(solution)/shard_map/all_to_all | solution.py:88
  238.5 114.2 %all-to-all-start.1 = ((bf16[16,3,4,2,8192]{4,3,2,1,0:T(2,128)(2,1)}), bf16[16,3,4,2,8192]{4,3,2,1,0:T(2,128)(2,1)}, u32[]{:S(2)}, u32[]{:S(2)}) async-start(bf16[16,3,4,2,8192]{4,3,2,1,0:T(2,128)(2,1)} %bitcast.51), calls=%async_computation.1 | async-start | bytes 12582912 | tf_op jit(solution)/shard_map/all_to_all | solution.py:88
Sparse Core Ops, SparseCore 0:
  12.5 52.0 all-gather.1
where the time goes:
time: 689 us; the launch traced here: 686 us
  matrix products  295 us (43%)
  waiting for transfers between devices  241 us (35%)
  local copies, waits for them, and re-layouts  93.2 us (14%)
  starting transfers between devices  21.5 us (3%)
  other arithmetic  20.5 us (3%)
  between operations  13.8 us (2%)
    all_to_all x2, waiting for transfers between devices, local(): lax.all_to_all(placed.astype(jnp.bfloat16).reshape(groups_count, MOST, pa...  189 us
    dot_general x16, matrix products, add_block(): jnp.dot(real_slice, cos_part, preferred_element_type=jnp.float32)  146 us
    dot_general x16, matrix products, add_block(): jnp.dot(imag_slice, sin_part, preferred_element_type=jnp.float32)  143 us
    all_gather x1, waiting for transfers between devices, local(): panel = lax.all_gather(white, 'chan', axis=0, tiled=True)  51.4 us
    convert_element_type x2, local copies, waits for them, and re-layouts, local(): placed.astype(jnp.bfloat16).reshape(groups_count, MOST, pairs, 2, F)  22 us
    all_to_all x2, starting transfers between devices, local(): lax.all_to_all(placed.astype(jnp.bfloat16).reshape(groups_count, MOST, pa...  21.5 us
  transfers between devices with their start and end apart: 3, of which 3 were waited for; matrix products, arithmetic and copies ran while one was open for 2% of the time, Pallas kernels for 0%

commit v1 on v0

--- a/solution.py
+++ b/solution.py
@@ -2,6 +2,7 @@
 import jax.numpy as jnp
 from jax import lax
 from jax.sharding import PartitionSpec as P
+from jax.lax import axis_index, ppermute, psum
 
 F = 8192
 LAGS = 1024
@@ -62,7 +63,14 @@
     groups_count = lax.axis_size("grp")
     slot_count = groups_count * MOST
     white = whiten(spectra)
-    panel = lax.all_gather(white, "chan", axis=0, tiled=True)
+    log = [white]
+    world = psum(1, "chan")
+    for t in range(world - 1):
+        clean = ppermute(log[-1], "chan", [(j, (j + 1) % world) for j in range(world)])
+        log.append(clean)
+    w_next = jnp.concatenate(log[::-1], 0)
+    part_now = axis_index("chan")
+    panel = jnp.roll(w_next, (part_now + 1) * white.shape[0], 0)
     blocks = pair_blocks[0, 0]
     offsets = jnp.arange(BLK, dtype=jnp.int32)
     left_idx = blocks[:, 0][:, None] * BLK + offsets

time: 689 us -> 746 us (1.083)
  the two profiles are of different devices: /device:TPU:20 before, /device:TPU:32 now
where the time goes in v1:
time: 746 us; the launch traced here: 739 us
  matrix products  295 us (40%)
  waiting for transfers between devices  263 us (35%)
  local copies, waits for them, and re-layouts  138 us (18%)
  other arithmetic  23.5 us (3%)
  starting transfers between devices  17.4 us (2%)
    all_to_all x2, waiting for transfers between devices, local(): lax.all_to_all(placed.astype(jnp.bfloat16).reshape(groups_count, MOST, pa...  164 us
    dot_general x16, matrix products, add_block(): jnp.dot(real_slice, cos_part, preferred_element_type=jnp.float32)  146 us
    dot_general x16, matrix products, add_block(): jnp.dot(imag_slice, sin_part, preferred_element_type=jnp.float32)  143 us
    ppermute x7, waiting for transfers between devices, local(): ppermute(log[-1], 'chan', [(j, (j + 1) % world) for j in range(world)])  99.1 us
    unnamed x44, local copies, waits for them, and re-layouts  32.9 us
    dynamic_slice x2, local copies, waits for them, and re-layouts, local(): panel = jnp.roll(w_next, (part_now + 1) * white.shape[0], 0)  24 us
    convert_element_type x2, local copies, waits for them, and re-layouts, local(): placed.astype(jnp.bfloat16).reshape(groups_count, MOST, pairs, 2, F)  22 us
    all_to_all x2, starting transfers between devices, local(): lax.all_to_all(placed.astype(jnp.bfloat16).reshape(groups_count, MOST, pa...  17.4 us
  transfers between devices with their start and end apart: 9, of which 9 were waited for; matrix products, arithmetic and copies ran while one was open for 2% of the time, Pallas kernels for 0%

profile of v1, /device:TPU:32, one launch (start us, length us, event | category | flops | bytes accessed | tf_op | source)
XLA Modules:
  0.0 738.6 jit_solution(8948296364902445074)
XLA Ops:
  3.7 14.2 %collective-permute-done = bf16[16,2,2,8192]{3,0,2,1:T(8,128)(2,1)S(1)} collective-permute-done((bf16[16,2,2,8192]{3,0,2,1:T(8,128)(2,1)S(1)}, bf16[16,2,2,8192]{3,0,2,1:T(8,128)(2,1)S(1)}, u32[]{:S(2)}, u32[]{:S(2)}) %collective-permute-start) | collective-permute-done | bytes 1048608 | tf_op jit(solution)/shard_map/ppermute | solution.py:69
  17.9 14.2 %collective-permute-done.1 = bf16[16,2,2,8192]{3,0,2,1:T(8,128)(2,1)S(1)} collective-permute-done((bf16[16,2,2,8192]{3,0,2,1:T(8,128)(2,1)S(1)}, bf16[16,2,2,8192]{3,0,2,1:T(8,128)(2,1)S(1)}, u32[]{:S(2)}, u32[]{:S(2)}) %collective-permute-start.1) | collective-permute-done | bytes 1048608 | tf_op jit(solution)/shard_map/ppermute | solution.py:69
  33.2 14.2 %collective-permute-done.2 = bf16[16,2,2,8192]{3,0,2,1:T(8,128)(2,1)S(1)} collective-permute-done((bf16[16,2,2,8192]{3,0,2,1:T(8,128)(2,1)S(1)}, bf16[16,2,2,8192]{3,0,2,1:T(8,128)(2,1)S(1)}, u32[]{:S(2)}, u32[]{:S(2)}) %collective-permute-start.2) | collective-permute-done | bytes 1048608 | tf_op jit(solution)/shard_map/ppermute | solution.py:69
  48.4 14.2 %collective-permute-done.3 = bf16[16,2,2,8192]{3,0,2,1:T(8,128)(2,1)S(1)} collective-permute-done((bf16[16,2,2,8192]{3,0,2,1:T(8,128)(2,1)S(1)}, bf16[16,2,2,8192]{3,0,2,1:T(8,128)(2,1)S(1)}, u32[]{:S(2)}, u32[]{:S(2)}) %collective-permute-start.3) | collective-permute-done | bytes 1048608 | tf_op jit(solution)/shard_map/ppermute | solution.py:69
  63.6 14.2 %collective-permute-done.4 = bf16[16,2,2,8192]{3,0,2,1:T(8,128)(2,1)S(1)} collective-permute-done((bf16[16,2,2,8192]{3,0,2,1:T(8,128)(2,1)S(1)}, bf16[16,2,2,8192]{3,0,2,1:T(8,128)(2,1)S(1)}, u32[]{:S(2)}, u32[]{:S(2)}) %collective-permute-start.4) | collective-permute-done | bytes 1048608 | tf_op jit(solution)/shard_map/ppermute | solution.py:69
  78.8 14.3 %collective-permute-done.5 = bf16[16,2,2,8192]{3,0,2,1:T(8,128)(2,1)} collective-permute-done((bf16[16,2,2,8192]{3,0,2,1:T(8,128)(2,1)S(1)}, bf16[16,2,2,8192]{3,0,2,1:T(8,128)(2,1)}, u32[]{:S(2)}, u32[]{:S(2)}) %collective-permute-start.5) | collective-permute-done | bytes 1048608 | tf_op jit(solution)/shard_map/ppermute | solution.py:69
  94.0 13.6 %collective-permute-done.6 = bf16[16,2,2,8192]{3,0,2,1:T(8,128)(2,1)} collective-permute-done((bf16[16,2,2,8192]{3,0,2,1:T(8,128)(2,1)}, bf16[16,2,2,8192]{3,0,2,1:T(8,128)(2,1)}, u32[]{:S(2)}, u32[]{:S(2)}) %collective-permute-start.6) | collective-permute-done | bytes 1048608 | tf_op jit(solution)/shard_map/ppermute | solution.py:69
  137.7 16.3 %copy.41 = bf16[128,2,2,8192]{3,2,1,0:T(2,128)(2,1)} copy(bf16[128,2,2,8192]{3,0,2,1:T(8,128)(2,1)} %constant_dynamic-slice_fusion) | data formatting | bytes 16777216 | tf_op jit(solution)/shard_map/jit(_roll_dynamic)/dynamic_slice | solution.py:73
  154.0 11.3 %gather_fusion = bf16[36,2,2,8192]{3,2,1,0:T(2,128)(2,1)S(1)} fusion(bf16[128,2,2,8192]{3,2,1,0:T(2,128)(2,1)} %copy.41, s32[1024]{0:T(1024)S(1)} %pad_clamp_fusion.1), kind=kCustom, calls=%fused_computation.clone | custom fusion | bytes 4718736 | tf_op jit(solution)/shard_map/jit(_take)/gather | solution.py:78
  179.4 11.5 %gather_fusion.1 = bf16[36,2,2,8192]{3,2,1,0:T(2,128)(2,1)S(1)} fusion(bf16[128,2,2,8192]{3,2,1,0:T(2,128)(2,1)} %copy.41, s32[1024]{0:T(1024)S(1)} %pad_clamp_fusion), kind=kCustom, calls=%fused_computation.1.clone | custom fusion | bytes 4718736 | tf_op jit(solution)/shard_map/jit(_take)/gather | solution.py:79
  205.7 11.0 %copy.49 = bf16[48,4,2,8192]{3,2,1,0:T(2,128)(2,1)} copy(bf16[48,4,2,8192]{3,0,2,1:T(8,128)(2,1)S(1)} %convolution_convert_fusion.1) | data formatting | bytes 12582912 | tf_op jit(solution)/shard_map/convert_element_type | solution.py:97
  227.1 11.0 %copy.50 = bf16[48,4,2,8192]{3,2,1,0:T(2,128)(2,1)} copy(bf16[48,4,2,8192]{3,0,2,1:T(8,128)(2,1)S(1)} %convolution_convert_fusion) | data formatting | bytes 12582912 | tf_op jit(solution)/shard_map/convert_element_type | solution.py:97
  238.1 85.4 %all-to-all-done = bf16[16,3,4,2,8192]{4,3,2,1,0:T(2,128)(2,1)} async-done(((bf16[16,3,4,2,8192]{4,3,2,1,0:T(2,128)(2,1)}), bf16[16,3,4,2,8192]{4,3,2,1,0:T(2,128)(2,1)}, u32[]{:S(2)}, u32[]{:S(2)}) %all-to-all-start) | async-done | bytes 6291488 | tf_op jit(solution)/shard_map/all_to_all | solution.py:96
  323.5 10.3 %all-to-all-start.1 = ((bf16[16,3,4,2,8192]{4,3,2,1,0:T(2,128)(2,1)}), bf16[16,3,4,2,8192]{4,3,2,1,0:T(2,128)(2,1)}, u32[]{:S(2)}, u32[]{:S(2)}) async-start(bf16[16,3,4,2,8192]{4,3,2,1,0:T(2,128)(2,1)} %bitcast.51), calls=%async_computation.1 | async-start | bytes 12582912 | tf_op jit(solution)/shard_map/all_to_all | solution.py:96
  333.9 78.6 %all-to-all-done.1 = bf16[16,3,4,2,8192]{4,3,2,1,0:T(2,128)(2,1)} async-done(((bf16[16,3,4,2,8192]{4,3,2,1,0:T(2,128)(2,1)}), bf16[16,3,4,2,8192]{4,3,2,1,0:T(2,128)(2,1)}, u32[]{:S(2)}, u32[]{:S(2)}) %all-to-all-start.1) | async-done | bytes 6291488 | tf_op jit(solution)/shard_map/all_to_all | solution.py:96
  412.4 11.2 %multiply_convert_fusion.4 = bf16[16,3,4,2,8192]{4,3,2,1,0:T(2,128)(2,1)S(1)} fusion(bf16[16,3,4,2,8192]{4,3,2,1,0:T(2,128)(2,1)} %all-to-all-done.1, bf16[16,3,4,2,8192]{4,3,2,1,0:T(2,128)(2,1)} %all-to-all-done), kind=kLoop, calls=%fused_computation.29 | loop fusion | flops 15728640 | bytes 18874368 | tf_op jit(solution)/shard_map/convert_element_type | solution.py:103
  423.6 13.4 %fusion.35 = (bf16[192,1,8192]{2,1,0:T(2,128)(2,1)S(1)}, bf16[192,1,8192]{2,1,0:T(2,128)(2,1)S(1)}) fusion(bf16[192,2,8192]{2,1,0:T(2,128)(2,1)S(1)} %bitcast.46), kind=kLoop, calls=%fused_computation.94 | loop fusion | bytes 12582912 | tf_op jit(solution)/shard_map/slice | solution.py:29
  445.6 290.4 %while.16 = (s32[]{:T(128)}, f32[192,1024]{1,0:T(8,128)}, bf16[192,8192]{1,0:T(8,128)(2,1)}, bf16[192,8192]{1,0:T(8,128)(2,1)S(1)}, s32[]{:T(128)}, /*index=5*/s32[]{:T(128)}, s32[]{:T(128)}, s32[]{:T(128)}) while((s32[]{:T(128)}, f32[192,1024]{1,0:T(8,128)}, bf16[192,8192]{1,0:T(8,128)(2,1)}, bf16[192,8192]{1,0:T(8,128)(2,1)S(1)}, ...), condition=%wide.region_3.5_spmd.clone, body=%wide.region_2.4_spmd.clone.sunk | while | flops 420548096 | bytes 3563677 | solution.py:40
  454.7 9.0 %convolution_add_fusion.5 = f32[192,1024]{1,0:T(8,128)} fusion(f32[192,1024]{1,0:T(8,128)S(1)} %convolution_add_fusion.4, f32[512]{0:T(512)S(1)} %select_multiply_fusion.2, s32[1024]{0:T(1024)S(1)} %iota_add_fusion.4, s32[512]{0:T(512)S(1)} %iota_add_fusion.5, bf16[192,8192]{1,0:T(8,128)(2,1)S(1)} %get-tuple-element.200, s32[]{:T(128)S(6)} %select_n.107), kind=kOutput, calls=%fused_computation.12.clone.1 | convolution fusion | flops 210436096 | bytes 1777668 | tf_op jit(solution)/shard_map/while/body/eval_jaxpr/dot_general | solution.py:37
  463.7 9.2 %convolution_add_fusion.4 = f32[192,1024]{1,0:T(8,128)S(1)} fusion(f32[512]{0:T(512)S(1)} %select_multiply_fusion.2, s32[1024]{0:T(1024)S(1)} %iota_add_fusion.4, s32[512]{0:T(512)S(1)} %iota_add_fusion.5, f32[192,1024]{1,0:T(8,128)} %get-tuple-element.190, pred[]{:T(512)S(6)} %compare.5, bf16[192,8192]{1,0:T(8,128)(2,1)} %get-tuple-element.199, ...), kind=kOutput, calls=%fused_computation.13.clone.1 | convolution fusion | flops 210108416 | bytes 1777669 | tf_op jit(solution)/shard_map/while/body/eval_jaxpr/dot_general | solution.py:36
  472.9 9.0 %convolution_add_fusion.5 = f32[192,1024]{1,0:T(8,128)} fusion(f32[192,1024]{1,0:T(8,128)S(1)} %convolution_add_fusion.4, f32[512]{0:T(512)S(1)} %select_multiply_fusion.2, s32[1024]{0:T(1024)S(1)} %iota_add_fusion.4, s32[512]{0:T(512)S(1)} %iota_add_fusion.5, bf16[192,8192]{1,0:T(8,128)(2,1)S(1)} %get-tuple-element.200, s32[]{:T(128)S(6)} %select_n.107), kind=kOutput, calls=%fused_computation.12.clone.1 | convolution fusion | flops 210436096 | bytes 1777668 | tf_op jit(solution)/shard_map/while/body/eval_jaxpr/dot_general | solution.py:37
  481.8 9.2 %convolution_add_fusion.4 = f32[192,1024]{1,0:T(8,128)S(1)} fusion(f32[512]{0:T(512)S(1)} %select_multiply_fusion.2, s32[1024]{0:T(1024)S(1)} %iota_add_fusion.4, s32[512]{0:T(512)S(1)} %iota_add_fusion.5, f32[192,1024]{1,0:T(8,128)} %get-tuple-element.190, pred[]{:T(512)S(6)} %compare.5, bf16[192,8192]{1,0:T(8,128)(2,1)} %get-tuple-element.199, ...), kind=kOutput, calls=%fused_computation.13.clone.1 | convolution fusion | flops 210108416 | bytes 1777669 | tf_op jit(solution)/shard_map/while/body/eval_jaxpr/dot_general | solution.py:36
  500.0 9.2 %convolution_add_fusion.4 = f32[192,1024]{1,0:T(8,128)S(1)} fusion(f32[512]{0:T(512)S(1)} %select_multiply_fusion.2, s32[1024]{0:T(1024)S(1)} %iota_add_fusion.4, s32[512]{0:T(512)S(1)} %iota_add_fusion.5, f32[192,1024]{1,0:T(8,128)} %get-tuple-element.190, pred[]{:T(512)S(6)} %compare.5, bf16[192,8192]{1,0:T(8,128)(2,1)} %get-tuple-element.199, ...), kind=kOutput, calls=%fused_computation.13.clone.1 | convolution fusion | flops 210108416 | bytes 1777669 | tf_op jit(solution)/shard_map/while/body/eval_jaxpr/dot_general | solution.py:36
  509.2 9.0 %convolution_add_fusion.5 = f32[192,1024]{1,0:T(8,128)} fusion(f32[192,1024]{1,0:T(8,128)S(1)} %convolution_add_fusion.4, f32[512]{0:T(512)S(1)} %select_multiply_fusion.2, s32[1024]{0:T(1024)S(1)} %iota_add_fusion.4, s32[512]{0:T(512)S(1)} %iota_add_fusion.5, bf16[192,8192]{1,0:T(8,128)(2,1)S(1)} %get-tuple-element.200, s32[]{:T(128)S(6)} %select_n.107), kind=kOutput, calls=%fused_computation.12.clone.1 | convolution fusion | flops 210436096 | bytes 1777668 | tf_op jit(solution)/shard_map/while/body/eval_jaxpr/dot_general | solution.py:37
  518.2 9.2 %convolution_add_fusion.4 = f32[192,1024]{1,0:T(8,128)S(1)} fusion(f32[512]{0:T(512)S(1)} %select_multiply_fusion.2, s32[1024]{0:T(1024)S(1)} %iota_add_fusion.4, s32[512]{0:T(512)S(1)} %iota_add_fusion.5, f32[192,1024]{1,0:T(8,128)} %get-tuple-element.190, pred[]{:T(512)S(6)} %compare.5, bf16[192,8192]{1,0:T(8,128)(2,1)} %get-tuple-element.199, ...), kind=kOutput, calls=%fused_computation.13.clone.1 | convolution fusion | flops 210108416 | bytes 1777669 | tf_op jit(solution)/shard_map/while/body/eval_jaxpr/dot_general | solution.py:36
  527.3 9.0 %convolution_add_fusion.5 = f32[192,1024]{1,0:T(8,128)} fusion(f32[192,1024]{1,0:T(8,128)S(1)} %convolution_add_fusion.4, f32[512]{0:T(512)S(1)} %select_multiply_fusion.2, s32[1024]{0:T(1024)S(1)} %iota_add_fusion.4, s32[512]{0:T(512)S(1)} %iota_add_fusion.5, bf16[192,8192]{1,0:T(8,128)(2,1)S(1)} %get-tuple-element.200, s32[]{:T(128)S(6)} %select_n.107), kind=kOutput, calls=%fused_computation.12.clone.1 | convolution fusion | flops 210436096 | bytes 1777668 | tf_op jit(solution)/shard_map/while/body/eval_jaxpr/dot_general | solution.py:37
  536.3 9.2 %convolution_add_fusion.4 = f32[192,1024]{1,0:T(8,128)S(1)} fusion(f32[512]{0:T(512)S(1)} %select_multiply_fusion.2, s32[1024]{0:T(1024)S(1)} %iota_add_fusion.4, s32[512]{0:T(512)S(1)} %iota_add_fusion.5, f32[192,1024]{1,0:T(8,128)} %get-tuple-element.190, pred[]{:T(512)S(6)} %compare.5, bf16[192,8192]{1,0:T(8,128)(2,1)} %get-tuple-element.199, ...), kind=kOutput, calls=%fused_computation.13.clone.1 | convolution fusion | flops 210108416 | bytes 1777669 | tf_op jit(solution)/shard_map/while/body/eval_jaxpr/dot_general | solution.py:36
  545.5 9.0 %convolution_add_fusion.5 = f32[192,1024]{1,0:T(8,128)} fusion(f32[192,1024]{1,0:T(8,128)S(1)} %convolution_add_fusion.4, f32[512]{0:T(512)S(1)} %select_multiply_fusion.2, s32[1024]{0:T(1024)S(1)} %iota_add_fusion.4, s32[512]{0:T(512)S(1)} %iota_add_fusion.5, bf16[192,8192]{1,0:T(8,128)(2,1)S(1)} %get-tuple-element.200, s32[]{:T(128)S(6)} %select_n.107), kind=kOutput, calls=%fused_computation.12.clone.1 | convolution fusion | flops 210436096 | bytes 1777668 | tf_op jit(solution)/shard_map/while/body/eval_jaxpr/dot_general | solution.py:37
  554.5 9.2 %convolution_add_fusion.4 = f32[192,1024]{1,0:T(8,128)S(1)} fusion(f32[512]{0:T(512)S(1)} %select_multiply_fusion.2, s32[1024]{0:T(1024)S(1)} %iota_add_fusion.4, s32[512]{0:T(512)S(1)} %iota_add_fusion.5, f32[192,1024]{1,0:T(8,128)} %get-tuple-element.190, pred[]{:T(512)S(6)} %compare.5, bf16[192,8192]{1,0:T(8,128)(2,1)} %get-tuple-element.199, ...), kind=kOutput, calls=%fused_computation.13.clone.1 | convolution fusion | flops 210108416 | bytes 1777669 | tf_op jit(solution)/shard_map/while/body/eval_jaxpr/dot_general | solution.py:36
  563.6 9.0 %convolution_add_fusion.5 = f32[192,1024]{1,0:T(8,128)} fusion(f32[192,1024]{1,0:T(8,128)S(1)} %convolution_add_fusion.4, f32[512]{0:T(512)S(1)} %select_multiply_fusion.2, s32[1024]{0:T(1024)S(1)} %iota_add_fusion.4, s32[512]{0:T(512)S(1)} %iota_add_fusion.5, bf16[192,8192]{1,0:T(8,128)(2,1)S(1)} %get-tuple-element.200, s32[]{:T(128)S(6)} %select_n.107), kind=kOutput, calls=%fused_computation.12.clone.1 | convolution fusion | flops 210436096 | bytes 1777668 | tf_op jit(solution)/shard_map/while/body/eval_jaxpr/dot_general | solution.py:37
  572.6 9.2 %convolution_add_fusion.4 = f32[192,1024]{1,0:T(8,128)S(1)} fusion(f32[512]{0:T(512)S(1)} %select_multiply_fusion.2, s32[1024]{0:T(1024)S(1)} %iota_add_fusion.4, s32[512]{0:T(512)S(1)} %iota_add_fusion.5, f32[192,1024]{1,0:T(8,128)} %get-tuple-element.190, pred[]{:T(512)S(6)} %compare.5, bf16[192,8192]{1,0:T(8,128)(2,1)} %get-tuple-element.199, ...), kind=kOutput, calls=%fused_computation.13.clone.1 | convolution fusion | flops 210108416 | bytes 1777669 | tf_op jit(solution)/shard_map/while/body/eval_jaxpr/dot_general | solution.py:36
  581.8 9.0 %convolution_add_fusion.5 = f32[192,1024]{1,0:T(8,128)} fusion(f32[192,1024]{1,0:T(8,128)S(1)} %convolution_add_fusion.4, f32[512]{0:T(512)S(1)} %select_multiply_fusion.2, s32[1024]{0:T(1024)S(1)} %iota_add_fusion.4, s32[512]{0:T(512)S(1)} %iota_add_fusion.5, bf16[192,8192]{1,0:T(8,128)(2,1)S(1)} %get-tuple-element.200, s32[]{:T(128)S(6)} %select_n.107), kind=kOutput, calls=%fused_computation.12.clone.1 | convolution fusion | flops 210436096 | bytes 1777668 | tf_op jit(solution)/shard_map/while/body/eval_jaxpr/dot_general | solution.py:37
  590.8 9.2 %convolution_add_fusion.4 = f32[192,1024]{1,0:T(8,128)S(1)} fusion(f32[512]{0:T(512)S(1)} %select_multiply_fusion.2, s32[1024]{0:T(1024)S(1)} %iota_add_fusion.4, s32[512]{0:T(512)S(1)} %iota_add_fusion.5, f32[192,1024]{1,0:T(8,128)} %get-tuple-element.190, pred[]{:T(512)S(6)} %compare.5, bf16[192,8192]{1,0:T(8,128)(2,1)} %get-tuple-element.199, ...), kind=kOutput, calls=%fused_computation.13.clone.1 | convolution fusion | flops 210108416 | bytes 1777669 | tf_op jit(solution)/shard_map/while/body/eval_jaxpr/dot_general | solution.py:36
  600.0 9.0 %convolution_add_fusion.5 = f32[192,1024]{1,0:T(8,128)} fusion(f32[192,1024]{1,0:T(8,128)S(1)} %convolution_add_fusion.4, f32[512]{0:T(512)S(1)} %select_multiply_fusion.2, s32[1024]{0:T(1024)S(1)} %iota_add_fusion.4, s32[512]{0:T(512)S(1)} %iota_add_fusion.5, bf16[192,8192]{1,0:T(8,128)(2,1)S(1)} %get-tuple-element.200, s32[]{:T(128)S(6)} %select_n.107), kind=kOutput, calls=%fused_computation.12.clone.1 | convolution fusion | flops 210436096 | bytes 1777668 | tf_op jit(solution)/shard_map/while/body/eval_jaxpr/dot_general | solution.py:37
  608.9 9.2 %convolution_add_fusion.4 = f32[192,1024]{1,0:T(8,128)S(1)} fusion(f32[512]{0:T(512)S(1)} %select_multiply_fusion.2, s32[1024]{0:T(1024)S(1)} %iota_add_fusion.4, s32[512]{0:T(512)S(1)} %iota_add_fusion.5, f32[192,1024]{1,0:T(8,128)} %get-tuple-element.190, pred[]{:T(512)S(6)} %compare.5, bf16[192,8192]{1,0:T(8,128)(2,1)} %get-tuple-element.199, ...), kind=kOutput, calls=%fused_computation.13.clone.1 | convolution fusion | flops 210108416 | bytes 1777669 | tf_op jit(solution)/shard_map/while/body/eval_jaxpr/dot_general | solution.py:36
  618.1 9.0 %convolution_add_fusion.5 = f32[192,1024]{1,0:T(8,128)} fusion(f32[192,1024]{1,0:T(8,128)S(1)} %convolution_add_fusion.4, f32[512]{0:T(512)S(1)} %select_multiply_fusion.2, s32[1024]{0:T(1024)S(1)} %iota_add_fusion.4, s32[512]{0:T(512)S(1)} %iota_add_fusion.5, bf16[192,8192]{1,0:T(8,128)(2,1)S(1)} %get-tuple-element.200, s32[]{:T(128)S(6)} %select_n.107), kind=kOutput, calls=%fused_computation.12.clone.1 | convolution fusion | flops 210436096 | bytes 1777668 | tf_op jit(solution)/shard_map/while/body/eval_jaxpr/dot_general | solution.py:37
  627.1 9.2 %convolution_add_fusion.4 = f32[192,1024]{1,0:T(8,128)S(1)} fusion(f32[512]{0:T(512)S(1)} %select_multiply_fusion.2, s32[1024]{0:T(1024)S(1)} %iota_add_fusion.4, s32[512]{0:T(512)S(1)} %iota_add_fusion.5, f32[192,1024]{1,0:T(8,128)} %get-tuple-element.190, pred[]{:T(512)S(6)} %compare.5, bf16[192,8192]{1,0:T(8,128)(2,1)} %get-tuple-element.199, ...), kind=kOutput, calls=%fused_computation.13.clone.1 | convolution fusion | flops 210108416 | bytes 1777669 | tf_op jit(solution)/shard_map/while/body/eval_jaxpr/dot_general | solution.py:36
  636.3 9.0 %convolution_add_fusion.5 = f32[192,1024]{1,0:T(8,128)} fusion(f32[192,1024]{1,0:T(8,128)S(1)} %convolution_add_fusion.4, f32[512]{0:T(512)S(1)} %select_multiply_fusion.2, s32[1024]{0:T(1024)S(1)} %iota_add_fusion.4, s32[512]{0:T(512)S(1)} %iota_add_fusion.5, bf16[192,8192]{1,0:T(8,128)(2,1)S(1)} %get-tuple-element.200, s32[]{:T(128)S(6)} %select_n.107), kind=kOutput, calls=%fused_computation.12.clone.1 | convolution fusion | flops 210436096 | bytes 1777668 | tf_op jit(solution)/shard_map/while/body/eval_jaxpr/dot_general | solution.py:37
  645.2 9.2 %convolution_add_fusion.4 = f32[192,1024]{1,0:T(8,128)S(1)} fusion(f32[512]{0:T(512)S(1)} %select_multiply_fusion.2, s32[1024]{0:T(1024)S(1)} %iota_add_fusion.4, s32[512]{0:T(512)S(1)} %iota_add_fusion.5, f32[192,1024]{1,0:T(8,128)} %get-tuple-element.190, pred[]{:T(512)S(6)} %compare.5, bf16[192,8192]{1,0:T(8,128)(2,1)} %get-tuple-element.199, ...), kind=kOutput, calls=%fused_computation.13.clone.1 | convolution fusion | flops 210108416 | bytes 1777669 | tf_op jit(solution)/shard_map/while/body/eval_jaxpr/dot_general | solution.py:36
  654.4 9.0 %convolution_add_fusion.5 = f32[192,1024]{1,0:T(8,128)} fusion(f32[192,1024]{1,0:T(8,128)S(1)} %convolution_add_fusion.4, f32[512]{0:T(512)S(1)} %select_multiply_fusion.2, s32[1024]{0:T(1024)S(1)} %iota_add_fusion.4, s32[512]{0:T(512)S(1)} %iota_add_fusion.5, bf16[192,8192]{1,0:T(8,128)(2,1)S(1)} %get-tuple-element.200, s32[]{:T(128)S(6)} %select_n.107), kind=kOutput, calls=%fused_computation.12.clone.1 | convolution fusion | flops 210436096 | bytes 1777668 | tf_op jit(solution)/shard_map/while/body/eval_jaxpr/dot_general | solution.py:37
  663.4 9.2 %convolution_add_fusion.4 = f32[192,1024]{1,0:T(8,128)S(1)} fusion(f32[512]{0:T(512)S(1)} %select_multiply_fusion.2, s32[1024]{0:T(1024)S(1)} %iota_add_fusion.4, s32[512]{0:T(512)S(1)} %iota_add_fusion.5, f32[192,1024]{1,0:T(8,128)} %get-tuple-element.190, pred[]{:T(512)S(6)} %compare.5, bf16[192,8192]{1,0:T(8,128)(2,1)} %get-tuple-element.199, ...), kind=kOutput, calls=%fused_computation.13.clone.1 | convolution fusion | flops 210108416 | bytes 1777669 | tf_op jit(solution)/shard_map/while/body/eval_jaxpr/dot_general | solution.py:36
  672.6 9.0 %convolution_add_fusion.5 = f32[192,1024]{1,0:T(8,128)} fusion(f32[192,1024]{1,0:T(8,128)S(1)} %convolution_add_fusion.4, f32[512]{0:T(512)S(1)} %select_multiply_fusion.2, s32[1024]{0:T(1024)S(1)} %iota_add_fusion.4, s32[512]{0:T(512)S(1)} %iota_add_fusion.5, bf16[192,8192]{1,0:T(8,128)(2,1)S(1)} %get-tuple-element.200, s32[]{:T(128)S(6)} %select_n.107), kind=kOutput, calls=%fused_computation.12.clone.1 | convolution fusion | flops 210436096 | bytes 1777668 | tf_op jit(solution)/shard_map/while/body/eval_jaxpr/dot_general | solution.py:37
  681.6 9.2 %convolution_add_fusion.4 = f32[192,1024]{1,0:T(8,128)S(1)} fusion(f32[512]{0:T(512)S(1)} %select_multiply_fusion.2, s32[1024]{0:T(1024)S(1)} %iota_add_fusion.4, s32[512]{0:T(512)S(1)} %iota_add_fusion.5, f32[192,1024]{1,0:T(8,128)} %get-tuple-element.190, pred[]{:T(512)S(6)} %compare.5, bf16[192,8192]{1,0:T(8,128)(2,1)} %get-tuple-element.199, ...), kind=kOutput, calls=%fused_computation.13.clone.1 | convolution fusion | flops 210108416 | bytes 1777669 | tf_op jit(solution)/shard_map/while/body/eval_jaxpr/dot_general | solution.py:36
  690.7 9.0 %convolution_add_fusion.5 = f32[192,1024]{1,0:T(8,128)} fusion(f32[192,1024]{1,0:T(8,128)S(1)} %convolution_add_fusion.4, f32[512]{0:T(512)S(1)} %select_multiply_fusion.2, s32[1024]{0:T(1024)S(1)} %iota_add_fusion.4, s32[512]{0:T(512)S(1)} %iota_add_fusion.5, bf16[192,8192]{1,0:T(8,128)(2,1)S(1)} %get-tuple-element.200, s32[]{:T(128)S(6)} %select_n.107), kind=kOutput, calls=%fused_computation.12.clone.1 | convolution fusion | flops 210436096 | bytes 1777668 | tf_op jit(solution)/shard_map/while/body/eval_jaxpr/dot_general | solution.py:37
  699.7 9.2 %convolution_add_fusion.4 = f32[192,1024]{1,0:T(8,128)S(1)} fusion(f32[512]{0:T(512)S(1)} %select_multiply_fusion.2, s32[1024]{0:T(1024)S(1)} %iota_add_fusion.4, s32[512]{0:T(512)S(1)} %iota_add_fusion.5, f32[192,1024]{1,0:T(8,128)} %get-tuple-element.190, pred[]{:T(512)S(6)} %compare.5, bf16[192,8192]{1,0:T(8,128)(2,1)} %get-tuple-element.199, ...), kind=kOutput, calls=%fused_computation.13.clone.1 | convolution fusion | flops 210108416 | bytes 1777669 | tf_op jit(solution)/shard_map/while/body/eval_jaxpr/dot_general | solution.py:36
  708.9 9.0 %convolution_add_fusion.5 = f32[192,1024]{1,0:T(8,128)} fusion(f32[192,1024]{1,0:T(8,128)S(1)} %convolution_add_fusion.4, f32[512]{0:T(512)S(1)} %select_multiply_fusion.2, s32[1024]{0:T(1024)S(1)} %iota_add_fusion.4, s32[512]{0:T(512)S(1)} %iota_add_fusion.5, bf16[192,8192]{1,0:T(8,128)(2,1)S(1)} %get-tuple-element.200, s32[]{:T(128)S(6)} %select_n.107), kind=kOutput, calls=%fused_computation.12.clone.1 | convolution fusion | flops 210436096 | bytes 1777668 | tf_op jit(solution)/shard_map/while/body/eval_jaxpr/dot_general | solution.py:37
  717.9 9.2 %convolution_add_fusion.4 = f32[192,1024]{1,0:T(8,128)S(1)} fusion(f32[512]{0:T(512)S(1)} %select_multiply_fusion.2, s32[1024]{0:T(1024)S(1)} %iota_add_fusion.4, s32[512]{0:T(512)S(1)} %iota_add_fusion.5, f32[192,1024]{1,0:T(8,128)} %get-tuple-element.190, pred[]{:T(512)S(6)} %compare.5, bf16[192,8192]{1,0:T(8,128)(2,1)} %get-tuple-element.199, ...), kind=kOutput, calls=%fused_computation.13.clone.1 | convolution fusion | flops 210108416 | bytes 1777669 | tf_op jit(solution)/shard_map/while/body/eval_jaxpr/dot_general | solution.py:36
  727.0 9.0 %convolution_add_fusion.5 = f32[192,1024]{1,0:T(8,128)} fusion(f32[192,1024]{1,0:T(8,128)S(1)} %convolution_add_fusion.4, f32[512]{0:T(512)S(1)} %select_multiply_fusion.2, s32[1024]{0:T(1024)S(1)} %iota_add_fusion.4, s32[512]{0:T(512)S(1)} %iota_add_fusion.5, bf16[192,8192]{1,0:T(8,128)(2,1)S(1)} %get-tuple-element.200, s32[]{:T(128)S(6)} %select_n.107), kind=kOutput, calls=%fused_computation.12.clone.1 | convolution fusion | flops 210436096 | bytes 1777668 | tf_op jit(solution)/shard_map/while/body/eval_jaxpr/dot_general | solution.py:37
  (136 shorter events, 106.4 us)
Async XLA Ops:
  1.8 1.2 copy-start.1
  2.1 91.0 %copy-start.12 = (s32[1,1,18,2]{2,3,1,0:T(2,128)S(1)}, s32[1,1,18,2]{2,3,1,0:T(2,128)}, u32[]{:S(2)}) copy-start(s32[1,1,18,2]{2,3,1,0:T(2,128)} %param.8) | copy-start | bytes 436
  2.1 91.7 %copy-start.13 = (s32[1,1,18,1]{2,3,1,0:T(1,128)S(1)}, s32[1,1,18,1]{2,3,1,0:T(1,128)}, u32[]{:S(2)}) copy-start(s32[1,1,18,1]{2,3,1,0:T(1,128)} %param.9) | copy-start | bytes 220
  3.7 14.2 %collective-permute-start = (bf16[16,2,2,8192]{3,0,2,1:T(8,128)(2,1)S(1)}, bf16[16,2,2,8192]{3,0,2,1:T(8,128)(2,1)S(1)}, u32[]{:S(2)}, u32[]{:S(2)}) collective-permute-start(bf16[16,2,2,8192]{3,0,2,1:T(8,128)(2,1)S(1)} %multiply_convert_fusion.5), channel_id=1, source_target_pairs={{0,1},{1,2},{2,3},{3,4},{4,5},{5,6},{6,7},{7,0},{8,9},{9,10},{10,1... | collective-permute-start | bytes 3145736 | tf_op jit(solution)/shard_map/ppermute | solution.py:69
  17.9 14.2 %collective-permute-start.1 = (bf16[16,2,2,8192]{3,0,2,1:T(8,128)(2,1)S(1)}, bf16[16,2,2,8192]{3,0,2,1:T(8,128)(2,1)S(1)}, u32[]{:S(2)}, u32[]{:S(2)}) collective-permute-start(bf16[16,2,2,8192]{3,0,2,1:T(8,128)(2,1)S(1)} %collective-permute-done), channel_id=1, source_target_pairs={{0,1},{1,2},{2,3},{3,4},{4,5},{5,6},{6,7},{7,0},{8,9},{9,10},{10,1... | collective-permute-start | bytes 3145736 | tf_op jit(solution)/shard_map/ppermute | solution.py:69
  32.2 1.0 copy-start.4
  33.2 14.2 %collective-permute-start.2 = (bf16[16,2,2,8192]{3,0,2,1:T(8,128)(2,1)S(1)}, bf16[16,2,2,8192]{3,0,2,1:T(8,128)(2,1)S(1)}, u32[]{:S(2)}, u32[]{:S(2)}) collective-permute-start(bf16[16,2,2,8192]{3,0,2,1:T(8,128)(2,1)S(1)} %collective-permute-done.1), channel_id=1, source_target_pairs={{0,1},{1,2},{2,3},{3,4},{4,5},{5,6},{6,7},{7,0},{8,9},{9,10},{10,1... | collective-permute-start | bytes 3145736 | tf_op jit(solution)/shard_map/ppermute | solution.py:69
  47.4 1.0 copy-start.6
  48.4 14.2 %collective-permute-start.3 = (bf16[16,2,2,8192]{3,0,2,1:T(8,128)(2,1)S(1)}, bf16[16,2,2,8192]{3,0,2,1:T(8,128)(2,1)S(1)}, u32[]{:S(2)}, u32[]{:S(2)}) collective-permute-start(bf16[16,2,2,8192]{3,0,2,1:T(8,128)(2,1)S(1)} %collective-permute-done.2), channel_id=1, source_target_pairs={{0,1},{1,2},{2,3},{3,4},{4,5},{5,6},{6,7},{7,0},{8,9},{9,10},{10,1... | collective-permute-start | bytes 3145736 | tf_op jit(solution)/shard_map/ppermute | solution.py:69
  62.6 1.0 copy-start.8
  63.6 14.2 %collective-permute-start.4 = (bf16[16,2,2,8192]{3,0,2,1:T(8,128)(2,1)S(1)}, bf16[16,2,2,8192]{3,0,2,1:T(8,128)(2,1)S(1)}, u32[]{:S(2)}, u32[]{:S(2)}) collective-permute-start(bf16[16,2,2,8192]{3,0,2,1:T(8,128)(2,1)S(1)} %collective-permute-done.3), channel_id=1, source_target_pairs={{0,1},{1,2},{2,3},{3,4},{4,5},{5,6},{6,7},{7,0},{8,9},{9,10},{10,1... | collective-permute-start | bytes 3145736 | tf_op jit(solution)/shard_map/ppermute | solution.py:69
  77.8 1.0 copy-start.10
  78.8 14.3 %collective-permute-start.5 = (bf16[16,2,2,8192]{3,0,2,1:T(8,128)(2,1)S(1)}, bf16[16,2,2,8192]{3,0,2,1:T(8,128)(2,1)}, u32[]{:S(2)}, u32[]{:S(2)}) collective-permute-start(bf16[16,2,2,8192]{3,0,2,1:T(8,128)(2,1)S(1)} %collective-permute-done.4), channel_id=1, source_target_pairs={{0,1},{1,2},{2,3},{3,4},{4,5},{5,6},{6,7},{7,0},{8,9},{9,10},{10,1... | collective-permute-start | bytes 3145736 | tf_op jit(solution)/shard_map/ppermute | solution.py:69
  93.1 14.5 %collective-permute-start.6 = (bf16[16,2,2,8192]{3,0,2,1:T(8,128)(2,1)}, bf16[16,2,2,8192]{3,0,2,1:T(8,128)(2,1)}, u32[]{:S(2)}, u32[]{:S(2)}) collective-permute-start(bf16[16,2,2,8192]{3,0,2,1:T(8,128)(2,1)} %collective-permute-done.5), channel_id=1, source_target_pairs={{0,1},{1,2},{2,3},{3,4},{4,5},{5,6},{6,7},{7,0},{8,9},{9,10},{10,1... | collective-permute-start | bytes 3145736 | tf_op jit(solution)/shard_map/ppermute | solution.py:69
  93.8 18.5 %copy-start.11 = (bf16[16,2,2,8192]{3,0,2,1:T(8,128)(2,1)S(1)}, bf16[16,2,2,8192]{3,0,2,1:T(8,128)(2,1)}, u32[]{:S(2)}) copy-start(bf16[16,2,2,8192]{3,0,2,1:T(8,128)(2,1)} %copy-done.10) | copy-start | bytes 3145732
  94.0 19.3 %copy-start.9 = (bf16[16,2,2,8192]{3,0,2,1:T(8,128)(2,1)S(1)}, bf16[16,2,2,8192]{3,0,2,1:T(8,128)(2,1)}, u32[]{:S(2)}) copy-start(bf16[16,2,2,8192]{3,0,2,1:T(8,128)(2,1)} %copy-done.8) | copy-start | bytes 3145732
  109.9 4.4 copy-start.7
  112.2 3.1 copy-start.5
  198.4 3.1 copy-start.3
  199.9 2.0 copy-start.2
  203.4 2.2 copy-start
  216.7 106.8 %all-to-all-start = ((bf16[16,3,4,2,8192]{4,3,2,1,0:T(2,128)(2,1)}), bf16[16,3,4,2,8192]{4,3,2,1,0:T(2,128)(2,1)}, u32[]{:S(2)}, u32[]{:S(2)}) async-start(bf16[16,3,4,2,8192]{4,3,2,1,0:T(2,128)(2,1)} %bitcast.52), calls=%async_computation | async-start | bytes 12582912 | tf_op jit(solution)/shard_map/all_to_all | solution.py:96
  323.5 88.9 %all-to-all-start.1 = ((bf16[16,3,4,2,8192]{4,3,2,1,0:T(2,128)(2,1)}), bf16[16,3,4,2,8192]{4,3,2,1,0:T(2,128)(2,1)}, u32[]{:S(2)}, u32[]{:S(2)}) async-start(bf16[16,3,4,2,8192]{4,3,2,1,0:T(2,128)(2,1)} %bitcast.51), calls=%async_computation.1 | async-start | bytes 12582912 | tf_op jit(solution)/shard_map/all_to_all | solution.py:96
